TPU v7x, 512 devices: a whole 4x8x8 slice. The times are simulated.
512 devices in a mesh: view: 8 (over z_hi, x), col: 64 (over y, z_lo, core).
Axes of the slice: x: 4, y: 8, z: 8 (z_hi: 2, z_lo: 4; z = z_hi * 4 + z_lo), core: 2. Of those that a mesh axis runs over, the one named last changes fastest.
Arguments:
- estimate: float32 [2048, 64, 128], P('col', 'view'), may hold values from 0.5 to 2
- observed: float32 [8, 2048, 64, 128], P('view', 'col'), may hold values from 0.5 to 2
- psf_taps: float32 [8, 3, 31], replicated, as said below
- intersection: int32 [8, 16], replicated, may hold values 0 or 1
Outputs:
- deconvolved: float32 [2048, 64, 128], P('col', 'view')
Inputs may be any that keep to these rules, and one draw needn't show every extreme that they name: `psf_taps`: every tap is positive.
All inputs are finite; a program needn't handle non-finite values.
Results may differ from a plain program's by a relative error of at most 0.0003.
Values sent between devices are 32-bit elements; how exact they have to be, the bound alone decides.
No kernel may reach another device: no remote copies, remote signals or barrier semaphores. Data moves between devices by JAX's collectives and lax.ppermute only.
A program may use at most 64 MiB of HBM per device.

v0:
```python
from functools import partial
import jax
import jax.numpy as jnp
from jax import lax
from jax.sharding import PartitionSpec as P

TX = 128
ITERS = 2
HIGH = lax.Precision.HIGHEST


def extended_2(block, sides, width):
    for axis, dim in sides:
        count = lax.axis_size(axis)
        forward = [(i, i + 1) for i in range(count - 1)]
        backward = [(target, source) for source, target in forward]
        low = lax.ppermute(
            lax.slice_in_dim(block, block.shape[dim] - width, None, axis=dim), axis, forward
        )
        high = lax.ppermute(lax.slice_in_dim(block, 0, width, axis=dim), axis, backward)
        block = jnp.concatenate([low, block, high], axis=dim)
    return block


def banded(kernel, length):
    tap_count = kernel.shape[0]
    half_width = (tap_count - 1) // 2
    offsets = jnp.arange(length)[:, None] - jnp.arange(length)[None, :] + half_width
    onehot = (offsets[:, :, None] == jnp.arange(tap_count)[None, None, :]).astype(jnp.float32)
    return jnp.einsum("iok,k->io", onehot, kernel, precision=HIGH)


def column_weights(kernel, length):
    return jnp.sum(banded(kernel, length), axis=0)


def row_matrix(kernel, row_count, row_span):
    tap_count = kernel.shape[-1]
    offsets = jnp.arange(row_span)[None, :] - jnp.arange(row_count)[:, None]
    onehot = (offsets[:, :, None] == jnp.arange(tap_count)[None, None, :]).astype(jnp.float32)
    return jnp.einsum("xjk,k->xj", onehot, kernel, precision=HIGH)


def along_rows(extended, kernel):
    row_span = extended.shape[0]
    row_count = row_span - (kernel.shape[0] - 1)
    matrix = row_matrix(kernel, row_count, row_span)
    flattened = extended.reshape(row_span, -1)
    result = jnp.dot(matrix, flattened, precision=HIGH)
    return result.reshape((row_count,) + extended.shape[1:])


def across(field, kernels):
    result = jnp.einsum("xyz,yw->xwz", field, banded(kernels[1], field.shape[1]), precision=HIGH)
    return jnp.dot(result, banded(kernels[2], field.shape[2]), precision=HIGH)


def view_masks(intersection, first_row, row_count, tile_rows):
    global_rows = first_row + jnp.arange(row_count, dtype=jnp.int32)
    tile_index = jnp.floor_divide(global_rows, tile_rows)
    onehot = (
        tile_index[:, None] == jnp.arange(intersection.shape[1], dtype=jnp.int32)[None, :]
    ).astype(jnp.float32)
    return jnp.dot(intersection.astype(jnp.float32), onehot.T, precision=HIGH)


def body(estimate, observed, psf_taps, intersection):
    slab_rows = observed.shape[1]
    full_width = observed.shape[2]
    depth = observed.shape[3]
    own_width = estimate.shape[1]
    view_index = lax.axis_index("view")
    col_index = lax.axis_index("col")
    first_row = col_index * slab_rows
    kernels = psf_taps / jnp.sum(psf_taps, axis=2, keepdims=True)
    mirrored = kernels[:, :, ::-1]
    halo_rows = (kernels.shape[2] - 1) // 2
    picker = (jnp.arange(kernels.shape[0], dtype=jnp.int32) == view_index).astype(jnp.float32)
    own_kernels = jnp.einsum("v,vdk->dk", picker, kernels, precision=HIGH)
    own_mirror = own_kernels[:, ::-1]
    masks_all = view_masks(intersection, first_row - halo_rows, slab_rows + 2 * halo_rows, TX)
    row_mats = jax.vmap(
        partial(row_matrix, row_count=slab_rows, row_span=slab_rows + 2 * halo_rows)
    )(mirrored[:, 0])
    weight_rows = jnp.einsum("vxj,vj->vx", row_mats, masks_all, precision=HIGH)
    weight_cols = jax.vmap(partial(column_weights, length=full_width))(mirrored[:, 1])
    weight_depth = jax.vmap(partial(column_weights, length=depth))(mirrored[:, 2])
    weight_full = jnp.einsum(
        "vx,vy,vz->xyz", weight_rows, weight_cols, weight_depth, precision=HIGH
    )
    weight_own = lax.dynamic_slice_in_dim(weight_full, view_index * own_width, own_width, 1)
    mask_outer = jnp.dot(picker, masks_all, precision=HIGH)
    mask_inner = mask_outer[halo_rows : halo_rows + slab_rows]
    image_used = observed[0]
    current = estimate
    for iteration in range(ITERS):
        full_estimate = lax.all_gather(current, "view", axis=1, tiled=True)
        extended = extended_2(full_estimate, (("col", 0),), halo_rows)
        blurred = across(along_rows(extended, own_kernels[0]), own_kernels)
        inside = mask_inner[:, None, None] > 0
        ratio = jnp.where(inside, image_used / jnp.where(inside, blurred, 1.0), 0.0)
        padded_ratio = extended_2(ratio, (("col", 0),), halo_rows)
        summed = lax.psum_scatter(
            across(along_rows(padded_ratio, own_mirror[0]), own_mirror),
            "view",
            scatter_dimension=1,
            tiled=True,
        )
        current = current * (summed + 1.0) / (weight_own + 1.0)
    return current


def solution(mesh):
    return jax.shard_map(
        body,
        mesh=mesh,
        in_specs=(P("col", "view", None), P("view", "col", None, None), P(), P()),
        out_specs=P("col", "view", None),
        check_vma=False,
    )
```

profile of v0, /device:TPU:8, one launch (start us, length us, event | category | flops | bytes accessed | tf_op | source)
XLA Modules:
  0.0 433.1 jit_solution(17454508880146930062)
XLA Ops:
  11.2 71.4 %all-gather.3.cloned.1.call-done = f32[32,64,128]{2,1,0:T(8,128)} async-done(((f32[32,8,128]{2,1,0:T(8,128)}), f32[32,64,128]{2,1,0:T(8,128)}) %all-gather.3.cloned.1.call-update) | async-done | bytes 1048592 | tf_op jit(solution)/shard_map/all_gather | solution.py:97
  83.9 1.9 collective-permute-start
  85.9 6.3 %collective-permute-start.1 = (f32[15,64,128]{2,1,0:T(8,128)S(1)}, f32[15,64,128]{2,1,0:T(8,128)}, u32[]{:S(2)}, u32[]{:S(2)}) collective-permute-start(f32[15,64,128]{2,1,0:T(8,128)S(1)} %get-tuple-element.12), channel_id=1, source_target_pairs={{1,0},{2,1},{3,2},{4,3},{5,4},{6,5},{7,6},{8,7},{9,8},{10,9},{11,1... | collective-permute-start | bytes 1474568 | tf_op jit(solution)/shard_map/ppermute | solution.py:20
  93.8 3.2 collective-permute-done
  97.0 1.5 collective-permute-done.1
  100.0 2.3 fusion.6
  102.3 1.6 convolution_bitcast_fusion.3
  105.0 5.3 %collective-permute-start.2 = (f32[15,64,128]{2,1,0:T(8,128)S(1)}, f32[15,64,128]{2,1,0:T(8,128)S(1)}, u32[]{:S(2)}, u32[]{:S(2)}) collective-permute-start(f32[15,64,128]{2,1,0:T(8,128)S(1)} %get-tuple-element.9), channel_id=1, source_target_pairs={{0,1},{1,2},{2,3},{3,4},{4,5},{5,6},{6,7},{7,8},{8,9},{9,10},{10,1... | collective-permute-start | bytes 1474568 | tf_op jit(solution)/shard_map/ppermute | solution.py:17
  110.3 3.4 collective-permute-start.3
  116.0 2.4 collective-permute-done.2
  118.3 1.5 collective-permute-done.3
  121.3 2.3 fusion.4
  123.6 1.6 convolution_bitcast_fusion.2
  125.2 2.0 fusion.67
  130.2 1.8 fusion.36
  132.1 89.4 %reduce-scatter.3.cloned.1.call-done = f32[32,8,128]{2,1,0:T(8,128)} async-done(((f32[32,64,128]{2,1,0:T(8,128)}), f32[32,8,128]{2,1,0:T(8,128)}) %reduce-scatter.3.cloned.1.call-update) | async-done | bytes 131088 | tf_op jit(solution)/shard_map/reduce_scatter | solution.py:103
  221.4 1.6 bitcast_divide_fusion.1
  223.1 65.0 %all-gather.5.cloned.1.call-done = f32[32,64,128]{2,1,0:T(8,128)} async-done(((f32[32,8,128]{2,1,0:T(8,128)}), f32[32,64,128]{2,1,0:T(8,128)}) %all-gather.5.cloned.1.call-update) | async-done | bytes 1048592 | tf_op jit(solution)/shard_map/all_gather | solution.py:97
  289.4 1.9 collective-permute-start.4
  291.4 6.6 %collective-permute-start.5 = (f32[15,64,128]{2,1,0:T(8,128)S(1)}, f32[15,64,128]{2,1,0:T(8,128)S(1)}, u32[]{:S(2)}, u32[]{:S(2)}) collective-permute-start(f32[15,64,128]{2,1,0:T(8,128)S(1)} %get-tuple-element.8), channel_id=1, source_target_pairs={{1,0},{2,1},{3,2},{4,3},{5,4},{6,5},{7,6},{8,7},{9,8},{10,9},{11,1... | collective-permute-start | bytes 1474568 | tf_op jit(solution)/shard_map/ppermute | solution.py:20
  297.9 4.6 %collective-permute-done.4 = f32[15,64,128]{2,1,0:T(8,128)S(1)} collective-permute-done((f32[15,64,128]{2,1,0:T(8,128)S(1)}, f32[15,64,128]{2,1,0:T(8,128)S(1)}, u32[]{:S(2)}, u32[]{:S(2)}) %collective-permute-start.4) | collective-permute-done | bytes 491552 | tf_op jit(solution)/shard_map/ppermute | solution.py:17
  302.5 1.5 collective-permute-done.5
  304.5 2.3 fusion.2
  306.8 1.6 convolution_bitcast_fusion.1
  309.6 5.2 %collective-permute-start.6 = (f32[15,64,128]{2,1,0:T(8,128)S(1)}, f32[15,64,128]{2,1,0:T(8,128)S(1)}, u32[]{:S(2)}, u32[]{:S(2)}) collective-permute-start(f32[15,64,128]{2,1,0:T(8,128)S(1)} %get-tuple-element.5), channel_id=1, source_target_pairs={{0,1},{1,2},{2,3},{3,4},{4,5},{5,6},{6,7},{7,8},{8,9},{9,10},{10,1... | collective-permute-start | bytes 1474568 | tf_op jit(solution)/shard_map/ppermute | solution.py:17
  314.7 3.3 collective-permute-start.7
  318.0 4.8 %collective-permute-done.6 = f32[15,64,128]{2,1,0:T(8,128)S(1)} collective-permute-done((f32[15,64,128]{2,1,0:T(8,128)S(1)}, f32[15,64,128]{2,1,0:T(8,128)S(1)}, u32[]{:S(2)}, u32[]{:S(2)}) %collective-permute-start.6) | collective-permute-done | bytes 491552 | tf_op jit(solution)/shard_map/ppermute | solution.py:17
  324.8 2.3 fusion
  327.1 1.6 convolution_bitcast_fusion
  328.8 2.0 fusion.68
  330.7 94.2 %reduce-scatter.5.cloned.1.call-done = f32[32,8,128]{2,1,0:T(8,128)} async-done(((f32[32,64,128]{2,1,0:T(8,128)}), f32[32,8,128]{2,1,0:T(8,128)}) %reduce-scatter.5.cloned.1.call-update) | async-done | bytes 131088 | tf_op jit(solution)/shard_map/reduce_scatter | solution.py:103
  424.9 1.6 bitcast_divide_fusion
  (81 shorter events, 21.6 us)
Async XLA Ops:
  6.5 76.1 %all-gather.3.cloned.1.call-start = ((), (), s32[]{:S(2)}) async-start(), calls=%async_computation.2 | async-start | bytes 1179648 | tf_op jit(solution)/shard_map/all_gather | solution.py:97
  7.3 214.2 %reduce-scatter.3.cloned.1.call-start = ((), (), s32[]{:S(2)}) async-start(), calls=%async_computation.3 | async-start | bytes 1179648 | tf_op jit(solution)/shard_map/reduce_scatter | solution.py:103
  10.6 103.6 %copy-start.4 = (pred[64,64,31]{1,0,2:T(32,128)(4,1)}, pred[64,64,31]{1,0,2:T(32,128)(4,1)S(1)}, u32[]{:S(2)}) copy-start(pred[64,64,31]{1,0,2:T(32,128)(4,1)S(1)} %iota_compare_fusion.1) | copy-start | bytes 380932
  11.2 91.1 %copy-start.6 = (f32[1,64,64]{2,0,1:T(1,128)}, f32[1,64,64]{2,0,1:T(1,128)S(1)}, u32[]{:S(2)}) copy-start(f32[1,64,64]{2,0,1:T(1,128)S(1)} %fusion.21) | copy-start | bytes 49156
  82.6 15.9 %copy-start = (f32[32,64,128]{2,1,0:T(8,128)S(1)}, f32[32,64,128]{2,1,0:T(8,128)}, u32[]{:S(2)}) copy-start(f32[32,64,128]{2,1,0:T(8,128)} %all-gather.3.cloned.1.call-done) | copy-start | bytes 3145732
  83.9 13.1 %collective-permute-start = (f32[15,64,128]{2,1,0:T(8,128)S(1)}, f32[15,64,128]{2,1,0:T(8,128)S(1)}, u32[]{:S(2)}, u32[]{:S(2)}) collective-permute-start(f32[15,64,128]{2,1,0:T(8,128)S(1)} %get-tuple-element.11), channel_id=1, source_target_pairs={{0,1},{1,2},{2,3},{3,4},{4,5},{5,6},{6,7},{7,8},{8,9},{9,10},{10,1... | collective-permute-start | bytes 1474568 | tf_op jit(solution)/shard_map/ppermute | solution.py:17
  85.9 12.7 %collective-permute-start.1 = (f32[15,64,128]{2,1,0:T(8,128)S(1)}, f32[15,64,128]{2,1,0:T(8,128)}, u32[]{:S(2)}, u32[]{:S(2)}) collective-permute-start(f32[15,64,128]{2,1,0:T(8,128)S(1)} %get-tuple-element.12), channel_id=1, source_target_pairs={{1,0},{2,1},{3,2},{4,3},{5,4},{6,5},{7,6},{8,7},{9,8},{10,9},{11,1... | collective-permute-start | bytes 1474568 | tf_op jit(solution)/shard_map/ppermute | solution.py:20
  100.0 3.9 copy-start.10
  105.0 13.3 %collective-permute-start.2 = (f32[15,64,128]{2,1,0:T(8,128)S(1)}, f32[15,64,128]{2,1,0:T(8,128)S(1)}, u32[]{:S(2)}, u32[]{:S(2)}) collective-permute-start(f32[15,64,128]{2,1,0:T(8,128)S(1)} %get-tuple-element.9), channel_id=1, source_target_pairs={{0,1},{1,2},{2,3},{3,4},{4,5},{5,6},{6,7},{7,8},{8,9},{9,10},{10,1... | collective-permute-start | bytes 1474568 | tf_op jit(solution)/shard_map/ppermute | solution.py:17
  110.3 9.6 %collective-permute-start.3 = (f32[15,64,128]{2,1,0:T(8,128)S(1)}, f32[15,64,128]{2,1,0:T(8,128)}, u32[]{:S(2)}, u32[]{:S(2)}) collective-permute-start(f32[15,64,128]{2,1,0:T(8,128)S(1)} %get-tuple-element.10), channel_id=1, source_target_pairs={{1,0},{2,1},{3,2},{4,3},{5,4},{6,5},{7,6},{8,7},{9,8},{10,9},{11,1... | collective-permute-start | bytes 1474568 | tf_op jit(solution)/shard_map/ppermute | solution.py:20
  114.8 8.8 %copy-start.8 = (f32[1,64,64]{2,0,1:T(1,128)}, f32[1,64,64]{2,0,1:T(1,128)S(1)}, u32[]{:S(2)}) copy-start(f32[1,64,64]{2,0,1:T(1,128)S(1)} %fusion.23) | copy-start | bytes 49156
  125.2 2.3 copy-start.5
  127.2 160.9 %all-gather.5.cloned.1.call-start = ((), (), s32[]{:S(2)}) async-start(), calls=%async_computation.4 | async-start | bytes 1179648 | tf_op jit(solution)/shard_map/all_gather | solution.py:97
  128.1 93.4 %copy-start.3 = (f32[32,8,128]{2,1,0:T(8,128)S(1)}, f32[32,8,128]{2,1,0:T(8,128)}, u32[]{:S(2)}) copy-start(f32[32,8,128]{2,1,0:T(8,128)} %param.4) | copy-start | bytes 393220
  223.1 201.9 %reduce-scatter.5.cloned.1.call-start = ((), (), s32[]{:S(2)}) async-start(), calls=%async_computation.5 | async-start | bytes 1179648 | tf_op jit(solution)/shard_map/reduce_scatter | solution.py:103
  288.1 16.0 %copy-start.1 = (f32[32,64,128]{2,1,0:T(8,128)S(1)}, f32[32,64,128]{2,1,0:T(8,128)}, u32[]{:S(2)}) copy-start(f32[32,64,128]{2,1,0:T(8,128)} %all-gather.5.cloned.1.call-done) | copy-start | bytes 3145732
  289.4 13.1 %collective-permute-start.4 = (f32[15,64,128]{2,1,0:T(8,128)S(1)}, f32[15,64,128]{2,1,0:T(8,128)S(1)}, u32[]{:S(2)}, u32[]{:S(2)}) collective-permute-start(f32[15,64,128]{2,1,0:T(8,128)S(1)} %get-tuple-element.7), channel_id=1, source_target_pairs={{0,1},{1,2},{2,3},{3,4},{4,5},{5,6},{6,7},{7,8},{8,9},{9,10},{10,1... | collective-permute-start | bytes 1474568 | tf_op jit(solution)/shard_map/ppermute | solution.py:17
  291.4 12.7 %collective-permute-start.5 = (f32[15,64,128]{2,1,0:T(8,128)S(1)}, f32[15,64,128]{2,1,0:T(8,128)S(1)}, u32[]{:S(2)}, u32[]{:S(2)}) collective-permute-start(f32[15,64,128]{2,1,0:T(8,128)S(1)} %get-tuple-element.8), channel_id=1, source_target_pairs={{1,0},{2,1},{3,2},{4,3},{5,4},{6,5},{7,6},{8,7},{9,8},{10,9},{11,1... | collective-permute-start | bytes 1474568 | tf_op jit(solution)/shard_map/ppermute | solution.py:20
  304.5 2.3 copy-start.7
  304.5 3.9 copy-start.11
  309.6 13.2 %collective-permute-start.6 = (f32[15,64,128]{2,1,0:T(8,128)S(1)}, f32[15,64,128]{2,1,0:T(8,128)S(1)}, u32[]{:S(2)}, u32[]{:S(2)}) collective-permute-start(f32[15,64,128]{2,1,0:T(8,128)S(1)} %get-tuple-element.5), channel_id=1, source_target_pairs={{0,1},{1,2},{2,3},{3,4},{4,5},{5,6},{6,7},{7,8},{8,9},{9,10},{10,1... | collective-permute-start | bytes 1474568 | tf_op jit(solution)/shard_map/ppermute | solution.py:17
  314.7 9.6 %collective-permute-start.7 = (f32[15,64,128]{2,1,0:T(8,128)S(1)}, f32[15,64,128]{2,1,0:T(8,128)S(1)}, u32[]{:S(2)}, u32[]{:S(2)}) collective-permute-start(f32[15,64,128]{2,1,0:T(8,128)S(1)} %get-tuple-element.6), channel_id=1, source_target_pairs={{1,0},{2,1},{3,2},{4,3},{5,4},{6,5},{7,6},{8,7},{9,8},{10,9},{11,1... | collective-permute-start | bytes 1474568 | tf_op jit(solution)/shard_map/ppermute | solution.py:20
  324.8 2.3 copy-start.9
  328.7 96.2 %copy-start.2 = (f32[32,8,128]{2,1,0:T(8,128)S(1)}, f32[32,8,128]{2,1,0:T(8,128)}, u32[]{:S(2)}) copy-start(f32[32,8,128]{2,1,0:T(8,128)} %bitcast_divide_fusion.1) | copy-start | bytes 393220
Sparse Core Ops, SparseCore 0:
  10.4 72.1 all-gather.2
  127.3 94.0 reduce-scatter.2
  225.0 63.0 all-gather.4
  330.9 94.0 reduce-scatter.4
where the time goes:
time: 434 us; the launch traced here: 433 us
  waiting for transfers between devices  342 us (79%)
  starting transfers between devices  34 us (8%)
  matrix products  30.9 us (7%)
  between operations  13.6 us (3%)
  other arithmetic  8.23 us (2%)
  local copies, waits for them, and re-layouts  4.58 us (1%)
    reduce_scatter x2, waiting for transfers between devices, body(): lax.psum_scatter(across(along_rows(padded_ratio, own_mirror[0]), own_mirr...  184 us
    all_gather x2, waiting for transfers between devices, body(): full_estimate = lax.all_gather(current, 'view', axis=1, tiled=True)  136 us
    ppermute x4, starting transfers between devices, extended_2(): lax.ppermute(lax.slice_in_dim(block, 0, width, axis=dim), axis, backward)  19.6 us
    ppermute x4, waiting for transfers between devices, extended_2(): lax.ppermute(lax.slice_in_dim(block, block.shape[dim] - width, None, axis...  14.9 us
    ppermute x4, starting transfers between devices, extended_2(): lax.ppermute(lax.slice_in_dim(block, block.shape[dim] - width, None, axis...  14.3 us
    dot_general x4, matrix products, along_rows(): result = jnp.dot(matrix, flattened, precision=HIGH)  9.19 us
  transfers between devices with their start and end apart: 12, of which 12 were waited for; matrix products, arithmetic and copies ran while one was open for 3% of the time, Pallas kernels for 0%

commit v1 on v0

--- a/solution.py
+++ b/solution.py
@@ -7,6 +7,15 @@
 TX = 128
 ITERS = 2
 HIGH = lax.Precision.HIGHEST
+assign_the_group = lambda piece_in: jnp.concatenate(
+    lax.all_to_all(
+        jnp.stack(lax.axis_size("view") * [piece_in], 0),
+        axis_name="view",
+        split_axis=0,
+        concat_axis=0,
+    ),
+    1,
+)
 
 
 def extended_2(block, sides, width):
@@ -94,7 +103,7 @@
     image_used = observed[0]
     current = estimate
     for iteration in range(ITERS):
-        full_estimate = lax.all_gather(current, "view", axis=1, tiled=True)
+        full_estimate = assign_the_group(current)
         extended = extended_2(full_estimate, (("col", 0),), halo_rows)
         blurred = across(along_rows(extended, own_kernels[0]), own_kernels)
         inside = mask_inner[:, None, None] > 0

time: 434 us -> 362 us (0.83)
  waiting for transfers between devices: 342 us -> 231 us
  blocking collectives: 0 us -> 30 us
  starting transfers between devices: 34 us -> 47 us
  other arithmetic: 8.23 us -> 3.69 us
    all_gather x2 -> x0, waiting for transfers between devices: 136 us -> none  [body(): full_estimate = lax.all_gather(current, 'view', axis=1, tiled=True)]
    all_to_all x0 -> x1, blocking collectives: none -> 30 us  [lax.all_to_all(jnp.stack(lax.axis_size('view') * [piece_in], 0), axis_nam...]
    all_to_all x0 -> x1, waiting for transfers between devices: none -> 27.6 us  [lax.all_to_all(jnp.stack(lax.axis_size('view') * [piece_in], 0), axis_nam...]
    all_to_all x0 -> x1, starting transfers between devices: none -> 12.7 us  [lax.all_to_all(jnp.stack(lax.axis_size('view') * [piece_in], 0), axis_nam...]
  transfers between devices with their start and end apart: 12 -> 11, of which waited for: 12 -> 11; matrix products, arithmetic and copies ran while one was open for 3% -> 3% of each run, Pallas kernels for 0% -> 0%
where the time goes in v1:
time: 362 us
  waiting for transfers between devices  231 us (64%)
  starting transfers between devices  47 us (13%)
  blocking collectives  30 us (8%)
  matrix products  28.9 us (8%)
  between operations  13.9 us (4%)
  local copies, waits for them, and re-layouts  7.69 us (2%)
  other arithmetic  3.69 us (1%)
    reduce_scatter x2, waiting for transfers between devices, body(): lax.psum_scatter(across(along_rows(padded_ratio, own_mirror[0]), own_mirr...  184 us
    all_to_all x1, blocking collectives, lax.all_to_all(jnp.stack(lax.axis_size('view') * [piece_in], 0), axis_nam...  30 us
    all_to_all x1, waiting for transfers between devices, lax.all_to_all(jnp.stack(lax.axis_size('view') * [piece_in], 0), axis_nam...  27.6 us
    ppermute x4, starting transfers between devices, extended_2(): lax.ppermute(lax.slice_in_dim(block, 0, width, axis=dim), axis, backward)  19.3 us
    ppermute x4, starting transfers between devices, extended_2(): lax.ppermute(lax.slice_in_dim(block, block.shape[dim] - width, None, axis...  14.9 us
    ppermute x4, waiting for transfers between devices, extended_2(): lax.ppermute(lax.slice_in_dim(block, block.shape[dim] - width, None, axis...  13.7 us
    all_to_all x1, starting transfers between devices, lax.all_to_all(jnp.stack(lax.axis_size('view') * [piece_in], 0), axis_nam...  12.7 us
    dot_general x4, matrix products, along_rows(): result = jnp.dot(matrix, flattened, precision=HIGH)  9.19 us
  transfers between devices with their start and end apart: 11, of which 11 were waited for; matrix products, arithmetic and copies ran while one was open for 3% of the time, Pallas kernels for 0%

profile of v1, /device:TPU:8, one launch (start us, length us, event | category | flops | bytes accessed | tf_op | source)
XLA Modules:
  0.0 361.9 jit_solution(15189771167026223360)
XLA Ops:
  6.5 2.0 stack.4
  8.5 12.7 %all-to-all-start = ((f32[8,32,8,128]{3,2,1,0:T(8,128)}), f32[8,32,8,128]{3,2,1,0:T(8,128)S(1)}, u32[]{:S(2)}, u32[]{:S(2)}) async-start(f32[8,32,8,128]{3,2,1,0:T(8,128)} %stack.4), calls=%async_computation | async-start | bytes 2097152 | tf_op jit(solution)/shard_map/all_to_all | solution.py:11
  22.4 27.6 %all-to-all-done = f32[8,32,8,128]{3,2,1,0:T(8,128)S(1)} async-done(((f32[8,32,8,128]{3,2,1,0:T(8,128)}), f32[8,32,8,128]{3,2,1,0:T(8,128)S(1)}, u32[]{:S(2)}, u32[]{:S(2)}) %all-to-all-start) | async-done | bytes 1048608 | tf_op jit(solution)/shard_map/all_to_all | solution.py:11
  50.2 1.9 collective-permute-start
  52.1 6.3 %collective-permute-start.1 = (f32[15,64,128]{2,1,0:T(8,128)S(1)}, f32[15,64,128]{2,1,0:T(8,128)S(1)}, u32[]{:S(2)}, u32[]{:S(2)}) collective-permute-start(f32[15,64,128]{2,1,0:T(8,128)S(1)} %get-tuple-element.14), channel_id=1, source_target_pairs={{1,0},{2,1},{3,2},{4,3},{5,4},{6,5},{7,6},{8,7},{9,8},{10,9},{11,1... | collective-permute-start | bytes 1474568 | tf_op jit(solution)/shard_map/ppermute | solution.py:29
  60.5 2.7 collective-permute-done
  66.0 2.3 fusion.6
  68.3 1.6 convolution_bitcast_fusion.3
  71.0 5.2 %collective-permute-start.2 = (f32[15,64,128]{2,1,0:T(8,128)S(1)}, f32[15,64,128]{2,1,0:T(8,128)S(1)}, u32[]{:S(2)}, u32[]{:S(2)}) collective-permute-start(f32[15,64,128]{2,1,0:T(8,128)S(1)} %get-tuple-element.11), channel_id=1, source_target_pairs={{0,1},{1,2},{2,3},{3,4},{4,5},{5,6},{6,7},{7,8},{8,9},{9,10},{10,1... | collective-permute-start | bytes 1474568 | tf_op jit(solution)/shard_map/ppermute | solution.py:26
  76.3 3.4 collective-permute-start.3
  81.5 2.8 collective-permute-done.2
  84.2 1.6 collective-permute-done.3
  86.2 2.3 fusion.4
  88.5 1.6 convolution_bitcast_fusion.2
  90.1 1.9 fusion.69
  94.7 1.8 fusion.38
  96.5 90.6 %reduce-scatter.3.cloned.1.call-done = f32[32,8,128]{2,1,0:T(8,128)} async-done(((f32[32,64,128]{2,1,0:T(8,128)}), f32[32,8,128]{2,1,0:T(8,128)}) %reduce-scatter.3.cloned.1.call-update) | async-done | bytes 131088 | tf_op jit(solution)/shard_map/reduce_scatter | solution.py:112
  188.1 30.0 %all_to_all.10 = f32[8,32,8,128]{3,2,1,0:T(8,128)S(1)} all-to-all(f32[8,32,8,128]{3,2,1,0:T(8,128)S(1)} %stack.5), channel_id=1, replica_groups=mesh['view'=8,'col'=64] {'view'}, dimensions={0} | all-to-all | bytes 2097152 | tf_op jit(solution)/shard_map/all_to_all | solution.py:11
  218.4 1.9 collective-permute-start.4
  220.3 6.6 %collective-permute-start.5 = (f32[15,64,128]{2,1,0:T(8,128)S(1)}, f32[15,64,128]{2,1,0:T(8,128)S(1)}, u32[]{:S(2)}, u32[]{:S(2)}) collective-permute-start(f32[15,64,128]{2,1,0:T(8,128)S(1)} %get-tuple-element.8), channel_id=1, source_target_pairs={{1,0},{2,1},{3,2},{4,3},{5,4},{6,5},{7,6},{8,7},{9,8},{10,9},{11,1... | collective-permute-start | bytes 1474568 | tf_op jit(solution)/shard_map/ppermute | solution.py:29
  227.5 3.9 %collective-permute-done.4 = f32[15,64,128]{2,1,0:T(8,128)S(1)} collective-permute-done((f32[15,64,128]{2,1,0:T(8,128)S(1)}, f32[15,64,128]{2,1,0:T(8,128)S(1)}, u32[]{:S(2)}, u32[]{:S(2)}) %collective-permute-start.4) | collective-permute-done | bytes 491552 | tf_op jit(solution)/shard_map/ppermute | solution.py:26
  234.2 2.3 fusion.2
  236.5 1.6 convolution_bitcast_fusion.1
  239.2 5.8 %collective-permute-start.6 = (f32[15,64,128]{2,1,0:T(8,128)S(1)}, f32[15,64,128]{2,1,0:T(8,128)S(1)}, u32[]{:S(2)}, u32[]{:S(2)}) collective-permute-start(f32[15,64,128]{2,1,0:T(8,128)S(1)} %get-tuple-element.5), channel_id=1, source_target_pairs={{0,1},{1,2},{2,3},{3,4},{4,5},{5,6},{6,7},{7,8},{8,9},{9,10},{10,1... | collective-permute-start | bytes 1474568 | tf_op jit(solution)/shard_map/ppermute | solution.py:26
  245.0 3.0 collective-permute-start.7
  248.0 4.4 %collective-permute-done.6 = f32[15,64,128]{2,1,0:T(8,128)S(1)} collective-permute-done((f32[15,64,128]{2,1,0:T(8,128)S(1)}, f32[15,64,128]{2,1,0:T(8,128)S(1)}, u32[]{:S(2)}, u32[]{:S(2)}) %collective-permute-start.6) | collective-permute-done | bytes 491552 | tf_op jit(solution)/shard_map/ppermute | solution.py:26
  252.4 1.7 collective-permute-done.7
  254.6 2.3 fusion
  256.9 1.6 convolution_bitcast_fusion
  258.5 1.9 fusion.70
  260.5 93.0 %reduce-scatter.5.cloned.1.call-done = f32[32,8,128]{2,1,0:T(8,128)} async-done(((f32[32,64,128]{2,1,0:T(8,128)}), f32[32,8,128]{2,1,0:T(8,128)}) %reduce-scatter.5.cloned.1.call-update) | async-done | bytes 131088 | tf_op jit(solution)/shard_map/reduce_scatter | solution.py:112
  353.5 1.6 bitcast_divide_fusion
  (78 shorter events, 18.0 us)
Async XLA Ops:
  6.5 14.8 %copy-start.1 = (f32[8,3,31]{2,0,1:T(8,128)S(1)}, f32[8,3,31]{2,0,1:T(8,128)}, u32[]{:S(2)}) copy-start(f32[8,3,31]{2,0,1:T(8,128)} %param.6) | copy-start | bytes 8932
  6.5 15.1 %copy-start.4 = (s32[8,16]{1,0:T(8,128)S(1)}, s32[8,16]{1,0:T(8,128)}, u32[]{:S(2)}) copy-start(s32[8,16]{1,0:T(8,128)} %param.7) | copy-start | bytes 1540
  8.5 41.5 %all-to-all-start = ((f32[8,32,8,128]{3,2,1,0:T(8,128)}), f32[8,32,8,128]{3,2,1,0:T(8,128)S(1)}, u32[]{:S(2)}, u32[]{:S(2)}) async-start(f32[8,32,8,128]{3,2,1,0:T(8,128)} %stack.4), calls=%async_computation | async-start | bytes 2097152 | tf_op jit(solution)/shard_map/all_to_all | solution.py:11
  21.3 165.9 %reduce-scatter.3.cloned.1.call-start = ((), (), s32[]{:S(2)}) async-start(), calls=%async_computation.4 | async-start | bytes 1179648 | tf_op jit(solution)/shard_map/reduce_scatter | solution.py:112
  50.2 13.0 %collective-permute-start = (f32[15,64,128]{2,1,0:T(8,128)S(1)}, f32[15,64,128]{2,1,0:T(8,128)S(1)}, u32[]{:S(2)}, u32[]{:S(2)}) collective-permute-start(f32[15,64,128]{2,1,0:T(8,128)S(1)} %get-tuple-element.13), channel_id=1, source_target_pairs={{0,1},{1,2},{2,3},{3,4},{4,5},{5,6},{6,7},{7,8},{8,9},{9,10},{10,1... | collective-permute-start | bytes 1474568 | tf_op jit(solution)/shard_map/ppermute | solution.py:26
  52.1 12.7 %collective-permute-start.1 = (f32[15,64,128]{2,1,0:T(8,128)S(1)}, f32[15,64,128]{2,1,0:T(8,128)S(1)}, u32[]{:S(2)}, u32[]{:S(2)}) collective-permute-start(f32[15,64,128]{2,1,0:T(8,128)S(1)} %get-tuple-element.14), channel_id=1, source_target_pairs={{1,0},{2,1},{3,2},{4,3},{5,4},{6,5},{7,6},{8,7},{9,8},{10,9},{11,1... | collective-permute-start | bytes 1474568 | tf_op jit(solution)/shard_map/ppermute | solution.py:29
  66.0 3.9 %copy-start.2 = (f32[1,32,64,128]{3,2,1,0:T(8,128)S(1)}, f32[1,32,64,128]{3,2,1,0:T(8,128)}, u32[]{:S(2)}) copy-start(f32[1,32,64,128]{3,2,1,0:T(8,128)} %param.5) | copy-start | bytes 3145732
  71.0 13.2 %collective-permute-start.2 = (f32[15,64,128]{2,1,0:T(8,128)S(1)}, f32[15,64,128]{2,1,0:T(8,128)S(1)}, u32[]{:S(2)}, u32[]{:S(2)}) collective-permute-start(f32[15,64,128]{2,1,0:T(8,128)S(1)} %get-tuple-element.11), channel_id=1, source_target_pairs={{0,1},{1,2},{2,3},{3,4},{4,5},{5,6},{6,7},{7,8},{8,9},{9,10},{10,1... | collective-permute-start | bytes 1474568 | tf_op jit(solution)/shard_map/ppermute | solution.py:26
  76.3 9.5 %collective-permute-start.3 = (f32[15,64,128]{2,1,0:T(8,128)S(1)}, f32[15,64,128]{2,1,0:T(8,128)S(1)}, u32[]{:S(2)}, u32[]{:S(2)}) collective-permute-start(f32[15,64,128]{2,1,0:T(8,128)S(1)} %get-tuple-element.12), channel_id=1, source_target_pairs={{1,0},{2,1},{3,2},{4,3},{5,4},{6,5},{7,6},{8,7},{9,8},{10,9},{11,1... | collective-permute-start | bytes 1474568 | tf_op jit(solution)/shard_map/ppermute | solution.py:29
  92.0 95.1 %copy-start = (f32[32,8,128]{2,1,0:T(8,128)S(1)}, f32[32,8,128]{2,1,0:T(8,128)}, u32[]{:S(2)}) copy-start(f32[32,8,128]{2,1,0:T(8,128)} %param.4) | copy-start | bytes 393220
  92.1 261.5 %reduce-scatter.5.cloned.1.call-start = ((), (), s32[]{:S(2)}) async-start(), calls=%async_computation.5 | async-start | bytes 1179648 | tf_op jit(solution)/shard_map/reduce_scatter | solution.py:112
  218.4 13.0 %collective-permute-start.4 = (f32[15,64,128]{2,1,0:T(8,128)S(1)}, f32[15,64,128]{2,1,0:T(8,128)S(1)}, u32[]{:S(2)}, u32[]{:S(2)}) collective-permute-start(f32[15,64,128]{2,1,0:T(8,128)S(1)} %get-tuple-element.7), channel_id=1, source_target_pairs={{0,1},{1,2},{2,3},{3,4},{4,5},{5,6},{6,7},{7,8},{8,9},{9,10},{10,1... | collective-permute-start | bytes 1474568 | tf_op jit(solution)/shard_map/ppermute | solution.py:26
  220.3 12.7 %collective-permute-start.5 = (f32[15,64,128]{2,1,0:T(8,128)S(1)}, f32[15,64,128]{2,1,0:T(8,128)S(1)}, u32[]{:S(2)}, u32[]{:S(2)}) collective-permute-start(f32[15,64,128]{2,1,0:T(8,128)S(1)} %get-tuple-element.8), channel_id=1, source_target_pairs={{1,0},{2,1},{3,2},{4,3},{5,4},{6,5},{7,6},{8,7},{9,8},{10,9},{11,1... | collective-permute-start | bytes 1474568 | tf_op jit(solution)/shard_map/ppermute | solution.py:29
  234.2 3.9 %copy-start.3 = (f32[1,32,64,128]{3,2,1,0:T(8,128)S(1)}, f32[1,32,64,128]{3,2,1,0:T(8,128)}, u32[]{:S(2)}) copy-start(f32[1,32,64,128]{3,2,1,0:T(8,128)} %param.5) | copy-start | bytes 3145732
  239.2 13.2 %collective-permute-start.6 = (f32[15,64,128]{2,1,0:T(8,128)S(1)}, f32[15,64,128]{2,1,0:T(8,128)S(1)}, u32[]{:S(2)}, u32[]{:S(2)}) collective-permute-start(f32[15,64,128]{2,1,0:T(8,128)S(1)} %get-tuple-element.5), channel_id=1, source_target_pairs={{0,1},{1,2},{2,3},{3,4},{4,5},{5,6},{6,7},{7,8},{8,9},{9,10},{10,1... | collective-permute-start | bytes 1474568 | tf_op jit(solution)/shard_map/ppermute | solution.py:26
  245.0 9.1 %collective-permute-start.7 = (f32[15,64,128]{2,1,0:T(8,128)S(1)}, f32[15,64,128]{2,1,0:T(8,128)S(1)}, u32[]{:S(2)}, u32[]{:S(2)}) collective-permute-start(f32[15,64,128]{2,1,0:T(8,128)S(1)} %get-tuple-element.6), channel_id=1, source_target_pairs={{1,0},{2,1},{3,2},{4,3},{5,4},{6,5},{7,6},{8,7},{9,8},{10,9},{11,1... | collective-permute-start | bytes 1474568 | tf_op jit(solution)/shard_map/ppermute | solution.py:29
Sparse Core Ops, SparseCore 0:
  92.2 94.8 reduce-scatter.2
  260.6 92.8 reduce-scatter.4
